TPU v7x, 128 devices: a whole 4x4x4 slice. The times are simulated.
128 devices in a mesh: region: 128 (over x, y, z, core).
Axes of the slice: x: 4, y: 4, z: 4, core: 2. Of those that a mesh axis runs over, the one named last changes fastest.
Arguments:
- node_feat: bfloat16 [65536, 512], P('region'), may hold values from -6 to 6
- edge_feat: bfloat16 [524288, 512], P('region'), may hold values from -6 to 6
- sender: int32 [524288], P('region'), may hold values from 0 to 2815, as said below
- receiver: int32 [524288], P('region'), may hold values from 0 to 512, as said below
- send_list: int32 [128, 8, 32], P('region'), may hold values from 16 to 511
- edge_w1: bfloat16 [1536, 512], replicated, may hold values from -0.15625 to 0.15625
- edge_b1: float32 [512], replicated, may hold values from -4 to 4
- edge_w2: bfloat16 [512, 512], replicated, may hold values from -0.25 to 0.25
- edge_b2: float32 [512], replicated, may hold values from -4 to 4
- edge_gain: float32 [512], replicated, may hold values from 0.5 to 1.5
- edge_shift: float32 [512], replicated, may hold values from -4 to 4
- node_w1: bfloat16 [1024, 512], replicated, may hold values from -0.1875 to 0.1875
- node_b1: float32 [512], replicated, may hold values from -4 to 4
- node_w2: bfloat16 [512, 512], replicated, may hold values from -0.25 to 0.25
- node_b2: float32 [512], replicated, may hold values from -4 to 4
- node_gain: float32 [512], replicated, may hold values from 0.5 to 1.5
- node_shift: float32 [512], replicated, may hold values from -4 to 4
Outputs:
- edge_out: bfloat16 [524288, 512], P('region')
- node_out: bfloat16 [65536, 512], P('region')
Inputs may be any that keep to these rules, and one draw needn't show every extreme that they name: `sender`: a row of the region's table as built in the first step; every region has slots pointing at row 0 and at the last row. `receiver`: non-decreasing within each region's 4096 slots; the value 512 marks an empty slot, and empty slots stand after the used ones; some region uses all its slots. `send_list`: entry [s, j, k] is a local index on region s of a node that s sends to its j-th neighbour.
All inputs are finite; a program needn't handle non-finite values.
Results may differ from a plain program's by a relative error of at most 0.0043.
Values may be sent and summed in bfloat16 or wider, within the bound.
No kernel may reach another device: no remote copies, remote signals or barrier semaphores. Data moves between devices by JAX's collectives and lax.ppermute only.
A program may use at most 128 MiB of HBM per device.

v0:
```python
import jax
import jax.numpy as jnp
from jax import lax
from jax.sharding import PartitionSpec as P

COARSE_DEV = 16


NEIGHBOUR_STEPS = (1, -1, 7, -7, 8, -8, 9, -9)


def from_behind(block, axis, distance):
    devices = range(lax.axis_size(axis))
    route = [((i - distance) % len(devices), i) for i in devices]
    return lax.ppermute(block, axis, route)


def finish(pre, w_second, b_second, gain, shift):
    hidden = jax.nn.silu(pre).astype(jnp.bfloat16)
    out = jnp.dot(hidden, w_second, preferred_element_type=jnp.float32) + b_second
    mean = jnp.mean(out, axis=-1, keepdims=True)
    var = jnp.mean((out - mean) ** 2, axis=-1, keepdims=True)
    return (out - mean) * lax.rsqrt(var + 1e-05) * gain + shift


def pick_rows(wanted_rows, source, block_size):
    total_rows = wanted_rows.shape[0]
    grouped = wanted_rows.reshape(total_rows // block_size, block_size)
    source_ids = jnp.arange(source.shape[0], dtype=jnp.int32)

    def select(group_rows):
        one_hot = (group_rows[:, None] == source_ids[None, :]).astype(source.dtype)
        return jnp.dot(one_hot, source, preferred_element_type=jnp.float32).astype(source.dtype)

    return lax.map(select, grouped).reshape(total_rows, source.shape[1])


def on_device(
    node_feat,
    edge_feat,
    sender,
    receiver,
    send_list,
    edge_w1,
    edge_b1,
    edge_w2,
    edge_b2,
    edge_gain,
    edge_shift,
    node_w1,
    node_b1,
    node_w2,
    node_b2,
    node_gain,
    node_shift,
):
    width = node_feat.shape[1]
    node_rows = node_feat.shape[0]
    edge_rows = edge_feat.shape[0]
    neighbours = send_list.shape[1]
    slots = send_list.shape[2]
    block_size = min(512, edge_rows)
    block_count = edge_rows // block_size
    coarse = node_feat[:COARSE_DEV]
    outgoing = jnp.take(node_feat, send_list[0].reshape(-1), axis=0).reshape(
        neighbours, slots, width
    )
    coarse_all = lax.all_gather(coarse, "region", axis=0, tiled=True)
    arrived = [
        from_behind(rows_out, "region", distance)
        for rows_out, distance in zip(list(outgoing), NEIGHBOUR_STEPS)
    ]
    halo = jnp.concatenate(arrived, axis=0)
    table = jnp.concatenate([node_feat, coarse_all, halo], axis=0)
    live = receiver < node_rows
    recv_index = jnp.minimum(receiver, node_rows - 1)
    sent_rows = pick_rows(sender, table, block_size)
    recv_rows = pick_rows(recv_index, node_feat, block_size)
    inputs = jnp.concatenate([edge_feat, sent_rows, recv_rows], axis=1)
    edge_pre = jnp.dot(inputs, edge_w1, preferred_element_type=jnp.float32) + edge_b1
    update = finish(edge_pre, edge_w2, edge_b2, edge_gain, edge_shift)
    edge_out = jnp.where(live[:, None], edge_feat.astype(jnp.float32) + update, 0.0).astype(
        jnp.bfloat16
    )
    node_ids = jnp.arange(node_rows, dtype=jnp.int32)

    def add_block(position, running):
        first_slot = position * block_size
        block_rows = lax.dynamic_slice_in_dim(edge_out, first_slot, block_size, 0)
        block_ids = lax.dynamic_slice_in_dim(receiver, first_slot, block_size, 0)
        one_hot = (node_ids[:, None] == block_ids[None, :]).astype(jnp.bfloat16)
        return running + jnp.dot(one_hot, block_rows, preferred_element_type=jnp.float32)

    summed = lax.fori_loop(0, block_count, add_block, jnp.zeros((node_rows, width), jnp.float32))
    aggregate = summed.astype(jnp.bfloat16)
    node_in = jnp.concatenate([node_feat, aggregate], axis=1)
    node_pre = jnp.dot(node_in, node_w1, preferred_element_type=jnp.float32) + node_b1
    node_update = finish(node_pre, node_w2, node_b2, node_gain, node_shift)
    node_out = (node_feat.astype(jnp.float32) + node_update).astype(jnp.bfloat16)
    return (edge_out, node_out)


def solution(mesh):
    in_specs = (
        P("region", None),
        P("region", None),
        P("region"),
        P("region"),
        P("region", None, None),
        P(),
        P(),
        P(),
        P(),
        P(),
        P(),
        P(),
        P(),
        P(),
        P(),
        P(),
        P(),
    )
    out_specs = (P("region", None), P("region", None))
    return jax.shard_map(
        on_device, mesh=mesh, in_specs=in_specs, out_specs=out_specs, check_vma=False
    )
```

profile of v0, /device:TPU:0, one launch (start us, length us, event | category | flops | bytes accessed | tf_op | source)
XLA Modules:
  0.0 195.6 jit_solution(12757138436500873263)
XLA Ops:
  10.2 2.3 %gather_fusion = bf16[256,512]{1,0:T(8,128)(2,1)S(1)} fusion(bf16[512,512]{1,0:T(8,128)(2,1)} %param.23, s32[1024]{0:T(1024)S(1)} %pad_clamp_fusion), kind=kCustom, calls=%fused_computation | custom fusion | bytes 525312 | tf_op jit(solution)/shard_map/jit(_take)/gather | solution.py:65
  12.8 8.3 %collective-permute-start.1 = (bf16[32,512]{1,0:T(8,128)(2,1)S(1)}, bf16[32,512]{1,0:T(8,128)(2,1)}, u32[]{:S(2)}, u32[]{:S(2)}) collective-permute-start(bf16[32,512]{1,0:T(8,128)(2,1)S(1)} %get-tuple-element.226), channel_id=1, source_target_pairs={{1,0},{2,1},{3,2},{4,3},{5,4},{6,5},{7,6},{8,7},{9,8},{10,9},{11,1... | collective-permute-start | bytes 98312 | tf_op jit(solution)/shard_map/ppermute | solution.py:15
  21.1 5.1 %collective-permute-start.3 = (bf16[32,512]{1,0:T(8,128)(2,1)S(1)}, bf16[32,512]{1,0:T(8,128)(2,1)S(1)}, u32[]{:S(2)}, u32[]{:S(2)}) collective-permute-start(bf16[32,512]{1,0:T(8,128)(2,1)S(1)} %get-tuple-element.224), channel_id=1, source_target_pairs={{7,0},{8,1},{9,2},{10,3},{11,4},{12,5},{13,6},{14,7},{15,8},{16,9}... | collective-permute-start | bytes 98312 | tf_op jit(solution)/shard_map/ppermute | solution.py:15
  26.2 2.0 %copy.20 = bf16[512,512]{0,1:T(8,128)(2,1)} copy(bf16[512,512]{1,0:T(8,128)(2,1)} %param.23) | data formatting | bytes 1048576 | tf_op args[0]
  28.3 6.4 %copy.19 = bf16[4096,512]{0,1:T(8,128)(2,1)} copy(bf16[4096,512]{1,0:T(8,128)(2,1)} %param.24) | data formatting | bytes 8388608 | tf_op args[1]
  35.5 2.3 %broadcast.84.clone = bf16[8,512,512]{2,1,0:T(8,128)(2,1)} broadcast(bf16[]{:T(256)} %constant.76.clone.1), dimensions={} | broadcast | bytes 4194306 | tf_op jit(solution)/shard_map/broadcast.9
  37.8 10.4 %while.37 = (s32[]{:T(128)}, bf16[8,512,512]{2,1,0:T(8,128)(2,1)}, s32[8,512]{1,0:T(8,128)S(1)}, bf16[512,512]{1,0:T(8,128)(2,1)S(1)}, s32[]{:T(128)}) while((s32[]{:T(128)}, bf16[8,512,512]{2,1,0:T(8,128)(2,1)}, s32[8,512]{1,0:T(8,128)S(1)}, bf16[512,512]{1,0:T(8,128)(2,1)S(1)}, s32[]{:T(128)}) %tuple.90), condition=%wide.region_3.4_spmd.clone, body=%wide.region_2.3_spmd.clone.sunk | while | flops 268959744 | bytes 1055297 | solution.py:35
  48.3 30.9 %all-gather.2.cloned.1.call-done = bf16[2048,512]{1,0:T(8,128)(2,1)} async-done(((bf16[16,512]{1,0:T(8,128)(2,1)}), bf16[2048,512]{1,0:T(8,128)(2,1)}) %all-gather.2.cloned.1.call-update) | async-done | bytes 2097168 | tf_op jit(solution)/shard_map/all_gather | solution.py:68
  79.1 3.1 %constant_dynamic-update-slice_fusion.8 = bf16[2816,512]{1,0:T(8,128)(2,1)} fusion(bf16[2816,512]{1,0:T(8,128)(2,1)} %constant_dynamic-update-slice_fusion.9, bf16[2048,512]{1,0:T(8,128)(2,1)} %all-gather.2.cloned.1.call-done), kind=kLoop, calls=%fused_computation.54 | loop fusion | bytes 4194304
  82.2 2.7 %collective-permute-start.5 = (bf16[32,512]{1,0:T(8,128)(2,1)S(1)}, bf16[32,512]{1,0:T(8,128)(2,1)S(1)}, u32[]{:S(2)}, u32[]{:S(2)}) collective-permute-start(bf16[32,512]{1,0:T(8,128)(2,1)S(1)} %get-tuple-element.222), channel_id=1, source_target_pairs={{8,0},{9,1},{10,2},{11,3},{12,4},{13,5},{14,6},{15,7},{16,8},{17,9... | collective-permute-start | bytes 98312 | tf_op jit(solution)/shard_map/ppermute | solution.py:15
  87.6 7.5 %collective-permute-start.7 = (bf16[32,512]{1,0:T(8,128)(2,1)S(1)}, bf16[32,512]{1,0:T(8,128)(2,1)S(1)}, u32[]{:S(2)}, u32[]{:S(2)}) collective-permute-start(bf16[32,512]{1,0:T(8,128)(2,1)S(1)} %get-tuple-element.220), channel_id=1, source_target_pairs={{9,0},{10,1},{11,2},{12,3},{13,4},{14,5},{15,6},{16,7},{17,8},{18,... | collective-permute-start | bytes 98312 | tf_op jit(solution)/shard_map/ppermute | solution.py:15
  99.5 2.3 %broadcast.84.clone.1 = bf16[8,512,512]{2,1,0:T(8,128)(2,1)} broadcast(bf16[]{:T(256)} %constant.76.clone.1), dimensions={} | broadcast | bytes 4194306 | tf_op jit(solution)/shard_map/broadcast.9
  101.8 34.7 %while.36 = (s32[]{:T(128)}, bf16[8,512,512]{2,1,0:T(8,128)(2,1)}, s32[8,512]{1,0:T(8,128)S(1)}, bf16[2816,512]{1,0:T(8,128)(2,1)}, s32[]{:T(128)}) while((s32[]{:T(128)}, bf16[8,512,512]{2,1,0:T(8,128)(2,1)}, s32[8,512]{1,0:T(8,128)S(1)}, bf16[2816,512]{1,0:T(8,128)(2,1)}, s32[]{:T(128)}) %tuple.82), condition=%wide.region_1.2_spmd.clone, body=%wide.region_0.1_spmd.clone.sunk | while | flops 1478098944 | bytes 3414593 | solution.py:35
  101.8 4.4 %fusion.63 = bf16[8,512,512]{2,1,0:T(8,128)(2,1)} fusion(bf16[8,512,512]{2,1,0:T(8,128)(2,1)} %get-tuple-element.328, s32[]{:T(128)} %get-tuple-element.327, bf16[2816,512]{1,0:T(8,128)(2,1)} %get-tuple-element.335, s32[512]{0:T(512)S(1)} %bitcast.34), kind=kOutput, calls=%fused_computation.9.clone.1 | convolution fusion | flops 1478098944 | bytes 3410432 | tf_op jit(solution)/shard_map/while/body/eval_jaxpr/dot_general | solution.py:33
  106.2 4.3 %fusion.63 = bf16[8,512,512]{2,1,0:T(8,128)(2,1)} fusion(bf16[8,512,512]{2,1,0:T(8,128)(2,1)} %get-tuple-element.328, s32[]{:T(128)} %get-tuple-element.327, bf16[2816,512]{1,0:T(8,128)(2,1)} %get-tuple-element.335, s32[512]{0:T(512)S(1)} %bitcast.34), kind=kOutput, calls=%fused_computation.9.clone.1 | convolution fusion | flops 1478098944 | bytes 3410432 | tf_op jit(solution)/shard_map/while/body/eval_jaxpr/dot_general | solution.py:33
  110.5 4.3 %fusion.63 = bf16[8,512,512]{2,1,0:T(8,128)(2,1)} fusion(bf16[8,512,512]{2,1,0:T(8,128)(2,1)} %get-tuple-element.328, s32[]{:T(128)} %get-tuple-element.327, bf16[2816,512]{1,0:T(8,128)(2,1)} %get-tuple-element.335, s32[512]{0:T(512)S(1)} %bitcast.34), kind=kOutput, calls=%fused_computation.9.clone.1 | convolution fusion | flops 1478098944 | bytes 3410432 | tf_op jit(solution)/shard_map/while/body/eval_jaxpr/dot_general | solution.py:33
  114.9 4.3 %fusion.63 = bf16[8,512,512]{2,1,0:T(8,128)(2,1)} fusion(bf16[8,512,512]{2,1,0:T(8,128)(2,1)} %get-tuple-element.328, s32[]{:T(128)} %get-tuple-element.327, bf16[2816,512]{1,0:T(8,128)(2,1)} %get-tuple-element.335, s32[512]{0:T(512)S(1)} %bitcast.34), kind=kOutput, calls=%fused_computation.9.clone.1 | convolution fusion | flops 1478098944 | bytes 3410432 | tf_op jit(solution)/shard_map/while/body/eval_jaxpr/dot_general | solution.py:33
  119.2 4.3 %fusion.63 = bf16[8,512,512]{2,1,0:T(8,128)(2,1)} fusion(bf16[8,512,512]{2,1,0:T(8,128)(2,1)} %get-tuple-element.328, s32[]{:T(128)} %get-tuple-element.327, bf16[2816,512]{1,0:T(8,128)(2,1)} %get-tuple-element.335, s32[512]{0:T(512)S(1)} %bitcast.34), kind=kOutput, calls=%fused_computation.9.clone.1 | convolution fusion | flops 1478098944 | bytes 3410432 | tf_op jit(solution)/shard_map/while/body/eval_jaxpr/dot_general | solution.py:33
  123.5 4.3 %fusion.63 = bf16[8,512,512]{2,1,0:T(8,128)(2,1)} fusion(bf16[8,512,512]{2,1,0:T(8,128)(2,1)} %get-tuple-element.328, s32[]{:T(128)} %get-tuple-element.327, bf16[2816,512]{1,0:T(8,128)(2,1)} %get-tuple-element.335, s32[512]{0:T(512)S(1)} %bitcast.34), kind=kOutput, calls=%fused_computation.9.clone.1 | convolution fusion | flops 1478098944 | bytes 3410432 | tf_op jit(solution)/shard_map/while/body/eval_jaxpr/dot_general | solution.py:33
  127.9 4.3 %fusion.63 = bf16[8,512,512]{2,1,0:T(8,128)(2,1)} fusion(bf16[8,512,512]{2,1,0:T(8,128)(2,1)} %get-tuple-element.328, s32[]{:T(128)} %get-tuple-element.327, bf16[2816,512]{1,0:T(8,128)(2,1)} %get-tuple-element.335, s32[512]{0:T(512)S(1)} %bitcast.34), kind=kOutput, calls=%fused_computation.9.clone.1 | convolution fusion | flops 1478098944 | bytes 3410432 | tf_op jit(solution)/shard_map/while/body/eval_jaxpr/dot_general | solution.py:33
  132.2 4.3 %fusion.63 = bf16[8,512,512]{2,1,0:T(8,128)(2,1)} fusion(bf16[8,512,512]{2,1,0:T(8,128)(2,1)} %get-tuple-element.328, s32[]{:T(128)} %get-tuple-element.327, bf16[2816,512]{1,0:T(8,128)(2,1)} %get-tuple-element.335, s32[512]{0:T(512)S(1)} %bitcast.34), kind=kOutput, calls=%fused_computation.9.clone.1 | convolution fusion | flops 1478098944 | bytes 3410432 | tf_op jit(solution)/shard_map/while/body/eval_jaxpr/dot_general | solution.py:33
  136.6 13.9 %add_reduce_fusion = (f32[4096]{0:T(1024)S(1)}, f32[4096,512]{0,1:T(8,128)}) fusion(f32[512]{0:T(512)S(1)} %copy-done.5, bf16[512,512]{1,0:T(8,128)(2,1)} %param.30, bf16[1536,512]{1,0:T(8,128)(2,1)S(1)} %copy-done, bf16[4096,512]{1,0:T(8,128)(2,1)} %bitcast.32, bf16[4096,512]{1,0:T(8,128)(2,1)} %bitcast.31, bf16[4096,512]{1,0:T(8,128)(2,1)} %param.24, ...), kind=kOutput, calls=%fused_computation.31 | convolution fusion | flops 8644456448 | bytes 23089152 | tf_op jit(solution)/shard_map/dot_general | solution.py:20
  150.5 4.9 %multiply_reduce_fusion = f32[4096]{0:T(1024)S(1)} fusion(f32[4096,512]{0,1:T(8,128)} %get-tuple-element.229, f32[4096]{0:T(1024)S(1)} %broadcast_multiply_fusion, f32[512]{0:T(512)S(1)} %copy-done.5), kind=kLoop, calls=%fused_computation.29 | loop fusion | flops 8384512 | bytes 8423424 | tf_op jit(solution)/shard_map/reduce_sum | solution.py:22
  156.3 6.5 %select_convert_fusion = bf16[4096,512]{0,1:T(8,128)(2,1)} fusion(bf16[4096,512]{0,1:T(8,128)(2,1)} %copy.19, f32[4096,512]{0,1:T(8,128)S(1)} %copy-done.1, f32[512]{0:T(512)S(1)} %copy-done.6, f32[512]{0:T(512)S(1)} %copy-done.7, f32[4096]{0:T(1024)S(1)} %add_rsqrt_fusion, f32[4096]{0:T(1024)S(1)} %broadcast_multiply_fusion, f32[512]{0:T(512)S(1)} %copy-done.5, ...), kind=kLoop, calls=%fused_computation.28 | loop fusion | flops 18874368 | bytes 16820224 | tf_op jit(solution)/shard_map/convert_element_type | solution.py:82
  162.8 6.4 %copy.22 = bf16[4096,512]{1,0:T(8,128)(2,1)} copy(bf16[4096,512]{0,1:T(8,128)(2,1)} %select_convert_fusion) | data formatting | bytes 8388608
  169.2 13.3 %while.38 = (s32[]{:T(128)}, f32[512,512]{1,0:T(8,128)S(1)}, s32[4096]{0:T(1024)S(1)}, bf16[4096,512]{1,0:T(8,128)(2,1)}, s32[]{:T(128)}, /*index=5*/s32[]{:T(128)}, s32[]{:T(128)}, s32[]{:T(128)}) while((s32[]{:T(128)}, f32[512,512]{1,0:T(8,128)S(1)}, s32[4096]{0:T(1024)S(1)}, bf16[4096,512]{1,0:T(8,128)(2,1)}, s32[]{:T(128)}, ...), condition=%wide.region_7.8_spmd.clone, body=%wide.region_6.7_spmd.clone.sunk | while | flops 269221888 | bytes 2627733 | solution.py:94
  169.2 1.6 convolution_add_fusion.4
  172.6 1.6 convolution_add_fusion.4
  175.9 1.6 convolution_add_fusion.4
  177.6 1.6 convolution_add_fusion.4
  179.2 1.6 convolution_add_fusion.4
  183.4 2.8 %fusion.48 = (f32[512]{0:T(512)S(1)}, f32[512,512]{0,1:T(8,128)S(1)}) fusion(f32[512]{0:T(512)S(1)} %copy-done.11, bf16[512,512]{1,0:T(8,128)(2,1)} %param.36, bf16[1024,512]{1,0:T(8,128)(2,1)} %param.34, bf16[512,512]{1,0:T(8,128)(2,1)} %convert_element_type.36, bf16[512,512]{1,0:T(8,128)(2,1)S(1)} %get-tuple-element.362, f32[512]{0:T(512)S(1)} %copy-done.12), kind=kOutput, calls=%fused_computation.71 | convolution fusion | flops 809500160 | bytes 3676160 | tf_op jit(solution)/shard_map/dot_general | solution.py:20
  (105 shorter events, 31.3 us)
Async XLA Ops:
  7.2 129.4 %copy-start = (bf16[1536,512]{1,0:T(8,128)(2,1)S(1)}, bf16[1536,512]{1,0:T(8,128)(2,1)}, u32[]{:S(2)}) copy-start(bf16[1536,512]{1,0:T(8,128)(2,1)} %param.28) | copy-start | bytes 4718596
  7.2 21.0 %copy-start.4 = (s32[4096]{0:T(1024)S(1)}, s32[4096]{0:T(1024)}, u32[]{:S(2)}) copy-start(s32[4096]{0:T(1024)} %param.25) | copy-start | bytes 49156
  7.2 21.0 %copy-start.3 = (s32[4096]{0:T(1024)S(1)}, s32[4096]{0:T(1024)}, u32[]{:S(2)}) copy-start(s32[4096]{0:T(1024)} %param.26) | copy-start | bytes 49156
  7.2 71.9 %all-gather.2.cloned.1.call-start = ((), (), s32[]{:S(2)}) async-start(), calls=%async_computation | async-start | bytes 2113536 | tf_op jit(solution)/shard_map/all_gather | solution.py:68
  12.7 69.5 %collective-permute-start = (bf16[32,512]{1,0:T(8,128)(2,1)S(1)}, bf16[32,512]{1,0:T(8,128)(2,1)}, u32[]{:S(2)}, u32[]{:S(2)}) collective-permute-start(bf16[32,512]{1,0:T(8,128)(2,1)S(1)} %get-tuple-element.227), channel_id=1, source_target_pairs={{127,0},{0,1},{1,2},{2,3},{3,4},{4,5},{5,6},{6,7},{7,8},{8,9},{9,1... | collective-permute-start | bytes 98312 | tf_op jit(solution)/shard_map/ppermute | solution.py:15
  12.8 73.5 %collective-permute-start.1 = (bf16[32,512]{1,0:T(8,128)(2,1)S(1)}, bf16[32,512]{1,0:T(8,128)(2,1)}, u32[]{:S(2)}, u32[]{:S(2)}) collective-permute-start(bf16[32,512]{1,0:T(8,128)(2,1)S(1)} %get-tuple-element.226), channel_id=1, source_target_pairs={{1,0},{2,1},{3,2},{4,3},{5,4},{6,5},{7,6},{8,7},{9,8},{10,9},{11,1... | collective-permute-start | bytes 98312 | tf_op jit(solution)/shard_map/ppermute | solution.py:15
  21.1 66.5 %collective-permute-start.2 = (bf16[32,512]{1,0:T(8,128)(2,1)S(1)}, bf16[32,512]{1,0:T(8,128)(2,1)}, u32[]{:S(2)}, u32[]{:S(2)}) collective-permute-start(bf16[32,512]{1,0:T(8,128)(2,1)S(1)} %get-tuple-element.225), channel_id=1, source_target_pairs={{121,0},{122,1},{123,2},{124,3},{125,4},{126,5},{127,6},{0,7},{1,8... | collective-permute-start | bytes 98312 | tf_op jit(solution)/shard_map/ppermute | solution.py:15
  21.1 75.4 %collective-permute-start.3 = (bf16[32,512]{1,0:T(8,128)(2,1)S(1)}, bf16[32,512]{1,0:T(8,128)(2,1)S(1)}, u32[]{:S(2)}, u32[]{:S(2)}) collective-permute-start(bf16[32,512]{1,0:T(8,128)(2,1)S(1)} %get-tuple-element.224), channel_id=1, source_target_pairs={{7,0},{8,1},{9,2},{10,3},{11,4},{12,5},{13,6},{14,7},{15,8},{16,9}... | collective-permute-start | bytes 98312 | tf_op jit(solution)/shard_map/ppermute | solution.py:15
  26.2 70.9 %collective-permute-start.4 = (bf16[32,512]{1,0:T(8,128)(2,1)S(1)}, bf16[32,512]{1,0:T(8,128)(2,1)S(1)}, u32[]{:S(2)}, u32[]{:S(2)}) collective-permute-start(bf16[32,512]{1,0:T(8,128)(2,1)S(1)} %get-tuple-element.223), channel_id=1, source_target_pairs={{120,0},{121,1},{122,2},{123,3},{124,4},{125,5},{126,6},{127,7},{0... | collective-permute-start | bytes 98312 | tf_op jit(solution)/shard_map/ppermute | solution.py:15
  28.3 6.4 %copy-start.2 = (bf16[512,512]{1,0:T(8,128)(2,1)S(1)}, bf16[512,512]{1,0:T(8,128)(2,1)}, u32[]{:S(2)}) copy-start(bf16[512,512]{1,0:T(8,128)(2,1)} %param.23) | copy-start | bytes 1572868
  82.2 15.5 %collective-permute-start.5 = (bf16[32,512]{1,0:T(8,128)(2,1)S(1)}, bf16[32,512]{1,0:T(8,128)(2,1)S(1)}, u32[]{:S(2)}, u32[]{:S(2)}) collective-permute-start(bf16[32,512]{1,0:T(8,128)(2,1)S(1)} %get-tuple-element.222), channel_id=1, source_target_pairs={{8,0},{9,1},{10,2},{11,3},{12,4},{13,5},{14,6},{15,7},{16,8},{17,9... | collective-permute-start | bytes 98312 | tf_op jit(solution)/shard_map/ppermute | solution.py:15
  86.3 12.1 %collective-permute-start.6 = (bf16[32,512]{1,0:T(8,128)(2,1)S(1)}, bf16[32,512]{1,0:T(8,128)(2,1)S(1)}, u32[]{:S(2)}, u32[]{:S(2)}) collective-permute-start(bf16[32,512]{1,0:T(8,128)(2,1)S(1)} %get-tuple-element.221), channel_id=1, source_target_pairs={{119,0},{120,1},{121,2},{122,3},{123,4},{124,5},{125,6},{126,7},{1... | collective-permute-start | bytes 98312 | tf_op jit(solution)/shard_map/ppermute | solution.py:15
  87.6 11.3 %collective-permute-start.7 = (bf16[32,512]{1,0:T(8,128)(2,1)S(1)}, bf16[32,512]{1,0:T(8,128)(2,1)S(1)}, u32[]{:S(2)}, u32[]{:S(2)}) collective-permute-start(bf16[32,512]{1,0:T(8,128)(2,1)S(1)} %get-tuple-element.220), channel_id=1, source_target_pairs={{9,0},{10,1},{11,2},{12,3},{13,4},{14,5},{15,6},{16,7},{17,8},{18,... | collective-permute-start | bytes 98312 | tf_op jit(solution)/shard_map/ppermute | solution.py:15
  101.8 34.7 %copy-start.5 = (f32[512]{0:T(512)S(1)}, f32[512]{0:T(512)}, u32[]{:S(2)}) copy-start(f32[512]{0:T(512)} %param.31) | copy-start | bytes 6148
  101.8 34.7 %copy-start.10 = (f32[512]{0:T(512)S(1)}, f32[512]{0:T(512)}, u32[]{:S(2)}) copy-start(f32[512]{0:T(512)} %param.29) | copy-start | bytes 6148
  150.5 5.8 %copy-start.1 = (f32[4096,512]{0,1:T(8,128)S(1)}, f32[4096,512]{0,1:T(8,128)}, u32[]{:S(2)}) copy-start(f32[4096,512]{0,1:T(8,128)} %get-tuple-element.229) | copy-start | bytes 25165828
  150.5 5.8 %copy-start.6 = (f32[512]{0:T(512)S(1)}, f32[512]{0:T(512)}, u32[]{:S(2)}) copy-start(f32[512]{0:T(512)} %param.33) | copy-start | bytes 6148
  150.5 5.8 %copy-start.7 = (f32[512]{0:T(512)S(1)}, f32[512]{0:T(512)}, u32[]{:S(2)}) copy-start(f32[512]{0:T(512)} %param.32) | copy-start | bytes 6148
  169.2 14.2 %copy-start.11 = (f32[512]{0:T(512)S(1)}, f32[512]{0:T(512)}, u32[]{:S(2)}) copy-start(f32[512]{0:T(512)} %param.37) | copy-start | bytes 6148
  169.2 14.2 %copy-start.12 = (f32[512]{0:T(512)S(1)}, f32[512]{0:T(512)}, u32[]{:S(2)}) copy-start(f32[512]{0:T(512)} %param.35) | copy-start | bytes 6148
  183.4 3.0 %copy-start.8 = (f32[512]{0:T(512)S(1)}, f32[512]{0:T(512)}, u32[]{:S(2)}) copy-start(f32[512]{0:T(512)} %param.39) | copy-start | bytes 6148
  183.4 3.0 %copy-start.9 = (f32[512]{0:T(512)S(1)}, f32[512]{0:T(512)}, u32[]{:S(2)}) copy-start(f32[512]{0:T(512)} %param.38) | copy-start | bytes 6148
Sparse Core Ops, SparseCore 0:
  11.1 67.9 all-gather.1
where the time goes:
time: 197 us; the launch traced here: 196 us
  matrix products  74.3 us (38%)
  local copies, waits for them, and re-layouts  38.4 us (19%)
  waiting for transfers between devices  30.9 us (16%)
  starting transfers between devices  23.6 us (12%)
  between operations  14.2 us (7%)
  other arithmetic  13.9 us (7%)
    dot_general x16, matrix products, select(): jnp.dot(one_hot, source, preferred_element_type=jnp.float32)  45.1 us
    all_gather x1, waiting for transfers between devices, on_device(): coarse_all = lax.all_gather(coarse, 'region', axis=0, tiled=True)  30.9 us
    unnamed x39, local copies, waits for them, and re-layouts  27.2 us
    ppermute x8, starting transfers between devices, from_behind(): return lax.ppermute(block, axis, route)  23.6 us
    dot_general x2, matrix products, finish(): jnp.dot(hidden, w_second, preferred_element_type=jnp.float32) + b_second  16.7 us
    dot_general x8, matrix products, add_block(): jnp.dot(one_hot, block_rows, preferred_element_type=jnp.float32)  12.5 us
    convert_element_type x1, other arithmetic, on_device(): jnp.where(live[:, None], edge_feat.astype(jnp.float32) + update, 0.0)  6.49 us
    reduce_sum x2, other arithmetic, finish(): var = jnp.mean((out - mean) ** 2, axis=-1, keepdims=True)  5.06 us
  transfers between devices with their start and end apart: 9, of which 1 were waited for; matrix products, arithmetic and copies ran while one was open for 18% of the time, Pallas kernels for 0%

commit v1 on v0

v1 whole, which is shorter than its diff:
```python
import functools

import jax
import jax.numpy as jnp
from jax import lax
from jax.experimental import pallas as pl
from jax.experimental.pallas import tpu as pltpu
from jax.sharding import PartitionSpec as P

COARSE_DEV = 16
BLOCK = 512
WINDOW = 128
PHASES = ((2, 1, 0), (0, 2, 1))


def coords_of(region):
    return [region >> 5 & 3, region >> 3 & 3, region >> 1 & 3, region & 1]


def region_of(x, y, z, core):
    return ((x * 4 + y) * 4 + z) * 2 + core


def ring_route(phase, step):
    route = []
    for region in range(128):
        place = coords_of(region)
        dim = PHASES[place[3]][phase]
        place[dim] = (place[dim] + step) % 4
        route.append((region, region_of(*place)))
    return route


def linear_route(step):
    return [(i, (i + step) % 128) for i in range(128)]


def gather_coarse(coarse):
    held = coarse
    for phase in range(3):
        parts = [held]
        parts += [lax.ppermute(held, "region", ring_route(phase, k)) for k in (1, 2, 3)]
        held = jnp.concatenate(parts, axis=0)
    other = lax.ppermute(held, "region", [(i, i ^ 1) for i in range(128)])
    return held, other


def coarse_places(index):
    me = lax.axis_index("region")
    mine = coords_of(me)
    row = index & 15
    theirs = coords_of(index >> 4)
    rel = [(mine[d] - theirs[d]) & 3 for d in range(3)]
    order = [(rel[c] * 16 + rel[b] * 4 + rel[a]) for a, b, c in PHASES]
    block = jnp.where(theirs[3] == 0, order[0], order[1])
    return jnp.where(theirs[3] == mine[3], 0, 1024) + block * 16 + row


def exchange_halo(rows):
    up = lax.ppermute(
        jnp.concatenate([rows[4], rows[6], rows[2]], 0), "region", linear_route(8)
    )
    down = lax.ppermute(
        jnp.concatenate([rows[5], rows[3], rows[7]], 0), "region", linear_route(-8)
    )
    right = lax.ppermute(
        jnp.concatenate([rows[0], up[32:64], down[32:64]], 0), "region", linear_route(1)
    )
    left = lax.ppermute(
        jnp.concatenate([rows[1], up[64:96], down[64:96]], 0), "region", linear_route(-1)
    )
    return up, down, right, left


def layer_norm_update(hidden, w_ref, b_ref, gain_ref, shift_ref):
    y = jnp.dot(hidden, w_ref[...], preferred_element_type=jnp.float32) + b_ref[...]
    mean = jnp.mean(y, axis=-1, keepdims=True)
    d = y - mean
    var = jnp.mean(d * d, axis=-1, keepdims=True)
    return d * lax.rsqrt(var + 1e-05) * gain_ref[...] + shift_ref[...]


def half_silu(u):
    return (u + u * jnp.tanh(u)).astype(jnp.bfloat16)


def layer_kernel(
    send_ref, recv_ref, live_ref,
    recv_row, edge, node, own, other, up, down, right, left,
    w1, b1, w2, b2, gain, shift, nw1, nb1, nw2, nb2, ngain, nshift,
    edge_out, node_out,
    ts, tr, g, acc,
):
    step = pl.program_id(0)

    def project(src, count, w_lo, dst, first, bias):
        for lo in range(0, count, 256):
            n = min(256, count - lo)
            res = jnp.dot(
                src[lo : lo + n, :], w1[w_lo : w_lo + 512, :],
                preferred_element_type=jnp.float32,
            )
            if bias is not None:
                res = res + bias[...]
            for j in range(4):
                dst[pl.ds((first + lo) * 4 + j, n, stride=4), :] = res[:, j * 128 : j * 128 + 128]

    @pl.when(step == 0)
    def _():
        acc[...] = jnp.zeros_like(acc)
        tr[512 * 4 :, :] = jnp.zeros((tr.shape[0] - 2048, 128), jnp.float32)
        project(node, 512, 1024, tr, 0, b1)
        project(node, 512, 512, ts, 0, None)
        project(own, 1024, 512, ts, 512, None)
        project(other, 1024, 512, ts, 1536, None)
        project(up, 96, 512, ts, 2560, None)
        project(down, 96, 512, ts, 2656, None)
        project(right, 96, 512, ts, 2752, None)
        project(left, 96, 512, ts, 2848, None)

    first = step * BLOCK

    def fetch(e, carry):
        s = pl.multiple_of(send_ref[first + e] * 4, 4)
        r = pl.multiple_of(recv_ref[first + e] * 4, 4)
        g[pl.ds(pl.multiple_of(e * 4, 4), 4), :] = ts[pl.ds(s, 4), :] + tr[pl.ds(r, 4), :]
        return carry

    lax.fori_loop(0, BLOCK, fetch, 0, unroll=16)

    feat = edge[...]
    pre = jnp.dot(feat, w1[0:512, :], preferred_element_type=jnp.float32)
    gathered = jnp.concatenate([g[pl.ds(j, BLOCK, stride=4), :] for j in range(4)], axis=1)
    hidden = half_silu(0.5 * (pre + gathered))
    update = layer_norm_update(hidden, w2, b2, gain, shift)
    slot = first + lax.broadcasted_iota(jnp.int32, (BLOCK, 1), 0)
    result = jnp.where(slot < live_ref[0], feat.astype(jnp.float32) + update, 0.0).astype(jnp.bfloat16)
    edge_out[...] = result

    low = recv_ref[first] >> 3 << 3
    high = recv_ref[first + BLOCK - 1]

    def add_window(k, carry):
        base = pl.multiple_of(low + k * WINDOW, 8)
        ids = base + lax.broadcasted_iota(jnp.int32, (WINDOW, BLOCK), 0)
        one_hot = jnp.where(ids == recv_row[0], 1.0, 0.0).astype(jnp.bfloat16)
        acc[pl.ds(base, WINDOW), :] += jnp.dot(one_hot, edge_out[...], preferred_element_type=jnp.float32)
        return carry

    lax.fori_loop(0, (high - low) // WINDOW + 1, add_window, 0)

    @pl.when(step == pl.num_programs(0) - 1)
    def _():
        feat = node[...]
        pre = (
            jnp.dot(feat, nw1[0:512, :], preferred_element_type=jnp.float32)
            + jnp.dot(acc[0:512, :].astype(jnp.bfloat16), nw1[512:1024, :], preferred_element_type=jnp.float32)
            + nb1[...]
        )
        update = layer_norm_update(half_silu(0.5 * pre), nw2, nb2, ngain, nshift)
        node_out[...] = (feat.astype(jnp.float32) + update).astype(jnp.bfloat16)


def on_device(
    node_feat, edge_feat, sender, receiver, send_list,
    edge_w1, edge_b1, edge_w2, edge_b2, edge_gain, edge_shift,
    node_w1, node_b1, node_w2, node_b2, node_gain, node_shift,
):
    ids = jnp.arange(512, dtype=jnp.int32)
    pick = (send_list.reshape(256, 1) == ids[None, :]).astype(jnp.bfloat16)
    rows = jnp.dot(pick, node_feat, preferred_element_type=jnp.float32).astype(jnp.bfloat16)
    rows = rows.reshape(8, 32, 512)
    own, other = gather_coarse(node_feat[:COARSE_DEV])
    up, down, right, left = exchange_halo(rows)

    h = sender - 2560
    slot = h >> 5
    starts = (2752, 2848, 2880, 2816, 2560, 2656, 2784, 2912)
    start = jnp.full_like(sender, starts[0])
    for j in range(1, 8):
        start = jnp.where(slot == j, starts[j], start)
    place = jnp.where(
        sender < 512,
        sender,
        jnp.where(sender < 2560, 512 + coarse_places(sender - 512), start + (h & 31)),
    )
    live = jnp.sum((receiver < 512).astype(jnp.int32)).reshape(1)

    blocks = 4096 // BLOCK
    whole = lambda a: pl.BlockSpec(a.shape, lambda i, *_: (0,) * a.ndim, pipeline_mode=pl.Buffered(1))
    row = lambda a: a.reshape(1, -1)
    fixed = [
        node_feat, own, other, up, down, right, left,
        edge_w1, row(edge_b1), edge_w2, row(edge_b2), row(edge_gain), row(edge_shift),
        node_w1, row(node_b1), node_w2, row(node_b2), row(node_gain), row(node_shift),
    ]
    return pl.pallas_call(
        layer_kernel,
        grid_spec=pltpu.PrefetchScalarGridSpec(
            num_scalar_prefetch=3,
            grid=(blocks,),
            in_specs=[
                pl.BlockSpec((1, 1, BLOCK), lambda i, *_: (i, 0, 0)),
                pl.BlockSpec((BLOCK, 512), lambda i, *_: (i, 0)),
            ]
            + [whole(a) for a in fixed],
            out_specs=[
                pl.BlockSpec((BLOCK, 512), lambda i, *_: (i, 0)),
                pl.BlockSpec((512, 512), lambda i, *_: (0, 0)),
            ],
            scratch_shapes=[
                pltpu.VMEM((2944 * 4, 128), jnp.float32),
                pltpu.VMEM((520 * 4, 128), jnp.float32),
                pltpu.VMEM((BLOCK * 4, 128), jnp.float32),
                pltpu.VMEM((640, 512), jnp.float32),
            ],
        ),
        out_shape=[
            jax.ShapeDtypeStruct((4096, 512), jnp.bfloat16),
            jax.ShapeDtypeStruct((512, 512), jnp.bfloat16),
        ],
    )(place, receiver, live, receiver.reshape(blocks, 1, BLOCK), edge_feat, *fixed)


def solution(mesh):
    sharded = {0: P("region", None), 1: P("region", None), 2: P("region"), 3: P("region"), 4: P("region", None, None)}
    in_specs = tuple(sharded.get(i, P()) for i in range(17))
    out_specs = (P("region", None), P("region", None))
    step = lambda *a: tuple(on_device(*a))
    return jax.shard_map(step, mesh=mesh, in_specs=in_specs, out_specs=out_specs, check_vma=False)
```

time: 197 us -> 80.3 us (0.41)
  matrix products: 74.3 us -> 1.39 us
  local copies, waits for them, and re-layouts: 38.4 us -> 2.62 us
  Pallas kernels: 0 us -> 32 us
  waiting for transfers between devices: 30.9 us -> 14.7 us
  between operations: 14.2 us -> 0.84 us
  other arithmetic: 13.9 us -> 1.32 us
  starting transfers between devices: 23.6 us -> 27.4 us
    dot_general x26 -> x1, matrix products: 74.3 us -> 1.39 us  [on_device(): jnp.dot(pick, node_feat, preferred_element_type=jnp.float32)]
    pallas_call x0 -> x1, Pallas kernels: none -> 32 us  [on_device(): pl.pallas_call(layer_kernel, grid_spec=pltpu.PrefetchScalarGridSpec(num_s...]
    all_gather x1 -> x0, waiting for transfers between devices: 30.9 us -> none  [on_device(): coarse_all = lax.all_gather(coarse, 'region', axis=0, tiled=True)]
    unnamed x39 -> x24, local copies, waits for them, and re-layouts: 27.2 us -> 1.8 us
    ppermute x8 -> x14, waiting for transfers between devices: 0.02 us -> 14.7 us  [the longest x9 11.1 us: gather_coarse(): lax.ppermute(held, 'region', ring_route(phase, k))]
    convert_element_type x3 -> x0, other arithmetic: 8.69 us -> none  [the longest x1 6.49 us: on_device(): jnp.where(live[:, None], edge_feat.astype(jnp.float32) + update, 0.0)]
    another operation x5 -> x0, local copies, waits for them, and re-layouts: 6.16 us -> none
    reduce_sum x2 -> x1, other arithmetic: 5.06 us -> 0.64 us  [on_device(): live = jnp.sum((receiver < 512).astype(jnp.int32)).reshape(1)]
  transfers between devices with their start and end apart: 9 -> 14, of which waited for: 1 -> 6; matrix products, arithmetic and copies ran while one was open for 18% -> 4% of each run, Pallas kernels for 0% -> 0%
where the time goes in v1:
time: 80.3 us
  Pallas kernels  32 us (40%)
  starting transfers between devices  27.4 us (34%)
  waiting for transfers between devices  14.7 us (18%)
  local copies, waits for them, and re-layouts  2.62 us (3%)
  matrix products  1.39 us (2%)
  other arithmetic  1.32 us (2%)
  between operations  0.84 us (1%)
    pallas_call x1, Pallas kernels, on_device(): pl.pallas_call(layer_kernel, grid_spec=pltpu.PrefetchScalarGridSpec(num_s...  32 us
    ppermute x9, starting transfers between devices, gather_coarse(): lax.ppermute(held, 'region', ring_route(phase, k))  16.9 us
    ppermute x9, waiting for transfers between devices, gather_coarse(): lax.ppermute(held, 'region', ring_route(phase, k))  11.1 us
    ppermute x1, starting transfers between devices, exchange_halo(): lax.ppermute(jnp.concatenate([rows[1], up[64:96], down[64:96]], 0), 'regi...  7.22 us
    ppermute x1, starting transfers between devices, exchange_halo(): lax.ppermute(jnp.concatenate([rows[5], rows[3], rows[7]], 0), 'region', l...  3.11 us
    ppermute x1, waiting for transfers between devices, exchange_halo(): lax.ppermute(jnp.concatenate([rows[5], rows[3], rows[7]], 0), 'region', l...  2.05 us
    unnamed x24, local copies, waits for them, and re-layouts  1.8 us
  transfers between devices with their start and end apart: 14, of which 6 were waited for; matrix products, arithmetic and copies ran while one was open for 4% of the time, Pallas kernels for 0%

profile of v1, /device:TPU:0, one launch (start us, length us, event | category | flops | bytes accessed | tf_op | source)
XLA Modules:
  0.0 80.3 jit_solution(8467853074437962353)
XLA Ops:
  0.6 0.0 copy-start.4
  0.7 0.7 constant_dynamic-update-slice_fusion.6
  1.4 4.1 %collective-permute-start.2 = (bf16[16,512]{1,0:T(8,128)(2,1)S(1)}, bf16[16,512]{1,0:T(8,128)(2,1)S(1)}, u32[]{:S(2)}, u32[]{:S(2)}) collective-permute-start(bf16[16,512]{1,0:T(8,128)(2,1)S(1)} %get-tuple-element.4), channel_id=1, source_target_pairs={{0,6},{1,97},{2,0},{3,99},{4,2},{5,101},{6,4},{7,103},{8,14},{9,10... | collective-permute-start | bytes 49160 | tf_op jit(solution)/shard_map/ppermute | solution.py:42
  5.5 1.3 %collective-permute-start = (bf16[16,512]{1,0:T(8,128)(2,1)S(1)}, bf16[16,512]{1,0:T(8,128)(2,1)S(1)}, u32[]{:S(2)}, u32[]{:S(2)}) collective-permute-start(bf16[16,512]{1,0:T(8,128)(2,1)S(1)} %get-tuple-element.4), channel_id=1, source_target_pairs={{0,2},{1,33},{2,4},{3,35},{4,6},{5,37},{6,0},{7,39},{8,10},{9,41},... | collective-permute-start | bytes 49160 | tf_op jit(solution)/shard_map/ppermute | solution.py:42
  6.8 0.8 eq.68
  7.6 1.4 %convolution_convert_fusion = bf16[256,512]{1,0:T(8,128)(2,1)S(1)} fusion(bf16[512,512]{1,0:T(8,128)(2,1)} %node.1, s32[256]{0:T(256)S(1)} %eq.68), kind=kOutput, calls=%fused_computation | convolution fusion | flops 134479872 | bytes 787456 | tf_op jit(solution)/shard_map/dot_general | solution.py:171
  9.0 0.0 collective-permute-done.2
  9.0 1.8 %collective-permute-done.1 = bf16[16,512]{1,0:T(8,128)(2,1)S(1)} collective-permute-done((bf16[16,512]{1,0:T(8,128)(2,1)S(1)}, bf16[16,512]{1,0:T(8,128)(2,1)S(1)}, u32[]{:S(2)}, u32[]{:S(2)}) %collective-permute-start.1) | collective-permute-done | bytes 16416 | tf_op jit(solution)/shard_map/ppermute | solution.py:42
  10.8 3.1 %collective-permute-start.5 = (bf16[64,512]{1,0:T(8,128)(2,1)S(1)}, bf16[64,512]{1,0:T(8,128)(2,1)S(1)}, u32[]{:S(2)}, u32[]{:S(2)}) collective-permute-start(bf16[64,512]{1,0:T(8,128)(2,1)S(1)} %pad_maximum_fusion.4), channel_id=1, source_target_pairs={{0,24},{1,7},{2,26},{3,1},{4,28},{5,3},{6,30},{7,5},{8,0},{9,15},{... | collective-permute-start | bytes 196616 | tf_op jit(solution)/shard_map/ppermute | solution.py:42
  13.9 0.6 collective-permute-start.4
  14.5 1.0 %collective-permute-start.3 = (bf16[64,512]{1,0:T(8,128)(2,1)S(1)}, bf16[64,512]{1,0:T(8,128)(2,1)S(1)}, u32[]{:S(2)}, u32[]{:S(2)}) collective-permute-start(bf16[64,512]{1,0:T(8,128)(2,1)S(1)} %pad_maximum_fusion.4), channel_id=1, source_target_pairs={{0,8},{1,3},{2,10},{3,5},{4,12},{5,7},{6,14},{7,1},{8,16},{9,11},{... | collective-permute-start | bytes 196616 | tf_op jit(solution)/shard_map/ppermute | solution.py:42
  15.5 4.9 %collective-permute-done.3 = bf16[64,512]{1,0:T(8,128)(2,1)S(1)} collective-permute-done((bf16[64,512]{1,0:T(8,128)(2,1)S(1)}, bf16[64,512]{1,0:T(8,128)(2,1)S(1)}, u32[]{:S(2)}, u32[]{:S(2)}) %collective-permute-start.3) | collective-permute-done | bytes 65568 | tf_op jit(solution)/shard_map/ppermute | solution.py:42
  20.4 3.5 %collective-permute-start.7 = (bf16[256,512]{1,0:T(8,128)(2,1)S(1)}, bf16[256,512]{1,0:T(8,128)(2,1)S(1)}, u32[]{:S(2)}, u32[]{:S(2)}) collective-permute-start(bf16[256,512]{1,0:T(8,128)(2,1)S(1)} %get-tuple-element.17), channel_id=1, source_target_pairs={{0,64},{1,17},{2,66},{3,19},{4,68},{5,21},{6,70},{7,23},{8,72},{9,... | collective-permute-start | bytes 786440 | tf_op jit(solution)/shard_map/ppermute | solution.py:42
  23.9 0.7 collective-permute-start.6
  24.6 2.6 %collective-permute-start.8 = (bf16[256,512]{1,0:T(8,128)(2,1)S(1)}, bf16[256,512]{1,0:T(8,128)(2,1)S(1)}, u32[]{:S(2)}, u32[]{:S(2)}) collective-permute-start(bf16[256,512]{1,0:T(8,128)(2,1)S(1)} %get-tuple-element.17), channel_id=1, source_target_pairs={{0,96},{1,25},{2,98},{3,27},{4,100},{5,29},{6,102},{7,31},{8,104},... | collective-permute-start | bytes 786440 | tf_op jit(solution)/shard_map/ppermute | solution.py:42
  27.2 0.1 collective-permute-start.10
  27.3 4.2 %collective-permute-done.6 = bf16[256,512]{1,0:T(8,128)(2,1)S(1)} collective-permute-done((bf16[256,512]{1,0:T(8,128)(2,1)S(1)}, bf16[256,512]{1,0:T(8,128)(2,1)S(1)}, u32[]{:S(2)}, u32[]{:S(2)}) %collective-permute-start.6) | collective-permute-done | bytes 262176 | tf_op jit(solution)/shard_map/ppermute | solution.py:42
  31.5 0.2 collective-permute-done.8
  31.8 0.1 collective-permute-start.9
  31.9 3.1 %collective-permute-start.11 = (bf16[96,512]{1,0:T(8,128)(2,1)S(1)}, bf16[96,512]{1,0:T(8,128)(2,1)S(1)}, u32[]{:S(2)}, u32[]{:S(2)}) collective-permute-start(bf16[96,512]{1,0:T(8,128)(2,1)S(1)} %pad_maximum_fusion.1), channel_id=1, source_target_pairs={{0,120},{1,121},{2,122},{3,123},{4,124},{5,125},{6,126},{7,127},{8... | collective-permute-start | bytes 294920 | tf_op jit(solution)/shard_map/ppermute | solution.py:63
  35.0 0.6 compare_select_fusion.send_ref
  35.7 0.0 collective-permute-done.10.up
  35.7 2.0 %collective-permute-done.11.down = bf16[96,512]{1,0:T(8,128)(2,1)S(1)} collective-permute-done((bf16[96,512]{1,0:T(8,128)(2,1)S(1)}, bf16[96,512]{1,0:T(8,128)(2,1)S(1)}, u32[]{:S(2)}, u32[]{:S(2)}) %collective-permute-start.11) | collective-permute-done | bytes 98336 | tf_op jit(solution)/shard_map/ppermute | solution.py:63
  37.7 0.1 collective-permute-start.12
  37.8 7.2 %collective-permute-start.13 = (bf16[96,512]{1,0:T(8,128)(2,1)S(1)}, bf16[96,512]{1,0:T(8,128)(2,1)S(1)}, u32[]{:S(2)}, u32[]{:S(2)}) collective-permute-start(bf16[96,512]{1,0:T(8,128)(2,1)S(1)} %pad_maximum_fusion.3), channel_id=1, source_target_pairs={{0,127},{1,0},{2,1},{3,2},{4,3},{5,4},{6,5},{7,6},{8,7},{9,8},{10,... | collective-permute-start | bytes 294920 | tf_op jit(solution)/shard_map/ppermute | solution.py:69
  45.1 0.6 convert_reduce_fusion
  45.7 1.6 %collective-permute-done.12.right = bf16[96,512]{1,0:T(8,128)(2,1)S(1)} collective-permute-done((bf16[96,512]{1,0:T(8,128)(2,1)S(1)}, bf16[96,512]{1,0:T(8,128)(2,1)S(1)}, u32[]{:S(2)}, u32[]{:S(2)}) %collective-permute-start.12) | collective-permute-done | bytes 98336 | tf_op jit(solution)/shard_map/ppermute | solution.py:66
  47.3 0.0 collective-permute-done.13.left
  47.3 0.6 copy-done.5
  47.9 0.0 copy-done.6
  48.0 0.3 copy-done.1
  48.3 32.0 %shard_map.176 = (bf16[4096,512]{1,0:T(8,128)(2,1)}, bf16[512,512]{1,0:T(8,128)(2,1)}) custom-call(s32[4096]{0:T(1024)} %compare_select_fusion.send_ref, s32[4096]{0:T(1024)} %recv_ref.1, s32[1]{0:T(128)} %bitcast.live_ref, s32[8,1,512]{2,1,0:T(1,128)} %bitcast.11, bf16[4096,512]{1,0:T(8,128)(2,1)} %edge.1, bf16[512,512]{1,0:T(8,128)(2,1)} %node.1, ...), custom_call_target="tpu_custom_call" | custom-call | tf_op jit(solution)/shard_map/pallas_call | solution.py:197
  (35 shorter events, 0.2 us)
Async XLA Ops:
  0.6 34.4 %copy-start.7 = (s32[4096]{0:T(1024)S(1)}, s32[4096]{0:T(1024)}, u32[]{:S(2)}) copy-start(s32[4096]{0:T(1024)} %param.19) | copy-start | bytes 49156
  0.6 44.4 %copy-start.4 = (s32[4096]{0:T(1024)S(1)}, s32[4096]{0:T(1024)}, u32[]{:S(2)}) copy-start(s32[4096]{0:T(1024)} %recv_ref.1) | copy-start | bytes 49156
  1.4 7.6 %collective-permute-start.2 = (bf16[16,512]{1,0:T(8,128)(2,1)S(1)}, bf16[16,512]{1,0:T(8,128)(2,1)S(1)}, u32[]{:S(2)}, u32[]{:S(2)}) collective-permute-start(bf16[16,512]{1,0:T(8,128)(2,1)S(1)} %get-tuple-element.4), channel_id=1, source_target_pairs={{0,6},{1,97},{2,0},{3,99},{4,2},{5,101},{6,4},{7,103},{8,14},{9,10... | collective-permute-start | bytes 49160 | tf_op jit(solution)/shard_map/ppermute | solution.py:42
  5.5 5.2 %collective-permute-start.1 = (bf16[16,512]{1,0:T(8,128)(2,1)S(1)}, bf16[16,512]{1,0:T(8,128)(2,1)S(1)}, u32[]{:S(2)}, u32[]{:S(2)}) collective-permute-start(bf16[16,512]{1,0:T(8,128)(2,1)S(1)} %get-tuple-element.4), channel_id=1, source_target_pairs={{0,4},{1,65},{2,6},{3,67},{4,0},{5,69},{6,2},{7,71},{8,12},{9,73},... | collective-permute-start | bytes 49160 | tf_op jit(solution)/shard_map/ppermute | solution.py:42
  5.5 5.2 %collective-permute-start = (bf16[16,512]{1,0:T(8,128)(2,1)S(1)}, bf16[16,512]{1,0:T(8,128)(2,1)S(1)}, u32[]{:S(2)}, u32[]{:S(2)}) collective-permute-start(bf16[16,512]{1,0:T(8,128)(2,1)S(1)} %get-tuple-element.4), channel_id=1, source_target_pairs={{0,2},{1,33},{2,4},{3,35},{4,6},{5,37},{6,0},{7,39},{8,10},{9,41},... | collective-permute-start | bytes 49160 | tf_op jit(solution)/shard_map/ppermute | solution.py:42
  10.8 9.6 %collective-permute-start.5 = (bf16[64,512]{1,0:T(8,128)(2,1)S(1)}, bf16[64,512]{1,0:T(8,128)(2,1)S(1)}, u32[]{:S(2)}, u32[]{:S(2)}) collective-permute-start(bf16[64,512]{1,0:T(8,128)(2,1)S(1)} %pad_maximum_fusion.4), channel_id=1, source_target_pairs={{0,24},{1,7},{2,26},{3,1},{4,28},{5,3},{6,30},{7,5},{8,0},{9,15},{... | collective-permute-start | bytes 196616 | tf_op jit(solution)/shard_map/ppermute | solution.py:42
  13.9 6.5 %collective-permute-start.4 = (bf16[64,512]{1,0:T(8,128)(2,1)S(1)}, bf16[64,512]{1,0:T(8,128)(2,1)S(1)}, u32[]{:S(2)}, u32[]{:S(2)}) collective-permute-start(bf16[64,512]{1,0:T(8,128)(2,1)S(1)} %pad_maximum_fusion.4), channel_id=1, source_target_pairs={{0,16},{1,5},{2,18},{3,7},{4,20},{5,1},{6,22},{7,3},{8,24},{9,13},... | collective-permute-start | bytes 196616 | tf_op jit(solution)/shard_map/ppermute | solution.py:42
  14.5 5.8 %collective-permute-start.3 = (bf16[64,512]{1,0:T(8,128)(2,1)S(1)}, bf16[64,512]{1,0:T(8,128)(2,1)S(1)}, u32[]{:S(2)}, u32[]{:S(2)}) collective-permute-start(bf16[64,512]{1,0:T(8,128)(2,1)S(1)} %pad_maximum_fusion.4), channel_id=1, source_target_pairs={{0,8},{1,3},{2,10},{3,5},{4,12},{5,7},{6,14},{7,1},{8,16},{9,11},{... | collective-permute-start | bytes 196616 | tf_op jit(solution)/shard_map/ppermute | solution.py:42
  20.4 11.1 %collective-permute-start.7 = (bf16[256,512]{1,0:T(8,128)(2,1)S(1)}, bf16[256,512]{1,0:T(8,128)(2,1)S(1)}, u32[]{:S(2)}, u32[]{:S(2)}) collective-permute-start(bf16[256,512]{1,0:T(8,128)(2,1)S(1)} %get-tuple-element.17), channel_id=1, source_target_pairs={{0,64},{1,17},{2,66},{3,19},{4,68},{5,21},{6,70},{7,23},{8,72},{9,... | collective-permute-start | bytes 786440 | tf_op jit(solution)/shard_map/ppermute | solution.py:42
  23.9 7.6 %collective-permute-start.6 = (bf16[256,512]{1,0:T(8,128)(2,1)S(1)}, bf16[256,512]{1,0:T(8,128)(2,1)S(1)}, u32[]{:S(2)}, u32[]{:S(2)}) collective-permute-start(bf16[256,512]{1,0:T(8,128)(2,1)S(1)} %get-tuple-element.17), channel_id=1, source_target_pairs={{0,32},{1,9},{2,34},{3,11},{4,36},{5,13},{6,38},{7,15},{8,40},{9,1... | collective-permute-start | bytes 786440 | tf_op jit(solution)/shard_map/ppermute | solution.py:42
  24.6 7.1 %collective-permute-start.8 = (bf16[256,512]{1,0:T(8,128)(2,1)S(1)}, bf16[256,512]{1,0:T(8,128)(2,1)S(1)}, u32[]{:S(2)}, u32[]{:S(2)}) collective-permute-start(bf16[256,512]{1,0:T(8,128)(2,1)S(1)} %get-tuple-element.17), channel_id=1, source_target_pairs={{0,96},{1,25},{2,98},{3,27},{4,100},{5,29},{6,102},{7,31},{8,104},... | collective-permute-start | bytes 786440 | tf_op jit(solution)/shard_map/ppermute | solution.py:42
  27.2 8.4 %collective-permute-start.10 = (bf16[96,512]{1,0:T(8,128)(2,1)S(1)}, bf16[96,512]{1,0:T(8,128)(2,1)S(1)}, u32[]{:S(2)}, u32[]{:S(2)}) collective-permute-start(bf16[96,512]{1,0:T(8,128)(2,1)S(1)} %pad_maximum_fusion), channel_id=1, source_target_pairs={{0,8},{1,9},{2,10},{3,11},{4,12},{5,13},{6,14},{7,15},{8,16},{9,17... | collective-permute-start | bytes 294920 | tf_op jit(solution)/shard_map/ppermute | solution.py:60
  31.8 15.5 %copy-start = (bf16[1024,512]{1,0:T(8,128)(2,1)}, bf16[1024,512]{1,0:T(8,128)(2,1)S(1)}, u32[]{:S(2)}) copy-start(bf16[1024,512]{1,0:T(8,128)(2,1)S(1)} %constant_dynamic-update-slice_fusion.7.own) | copy-start | bytes 3145732
  31.8 15.5 %collective-permute-start.9 = (bf16[1024,512]{1,0:T(8,128)(2,1)S(1)}, bf16[1024,512]{1,0:T(8,128)(2,1)S(1)}, u32[]{:S(2)}, u32[]{:S(2)}) collective-permute-start(bf16[1024,512]{1,0:T(8,128)(2,1)S(1)} %constant_dynamic-update-slice_fusion.7.own), channel_id=1, source_target_pairs={{0,1},{1,0},{2,3},{3,2},{4,5},{5,4},{6,7},{7,6},{8,9},{9,8},{10,11... | collective-permute-start | bytes 3145736 | tf_op jit(solution)/shard_map/ppermute | solution.py:44
  31.9 5.8 %collective-permute-start.11 = (bf16[96,512]{1,0:T(8,128)(2,1)S(1)}, bf16[96,512]{1,0:T(8,128)(2,1)S(1)}, u32[]{:S(2)}, u32[]{:S(2)}) collective-permute-start(bf16[96,512]{1,0:T(8,128)(2,1)S(1)} %pad_maximum_fusion.1), channel_id=1, source_target_pairs={{0,120},{1,121},{2,122},{3,123},{4,124},{5,125},{6,126},{7,127},{8... | collective-permute-start | bytes 294920 | tf_op jit(solution)/shard_map/ppermute | solution.py:63
  35.7 11.7 %copy-start.2 = (bf16[96,512]{1,0:T(8,128)(2,1)}, bf16[96,512]{1,0:T(8,128)(2,1)S(1)}, u32[]{:S(2)}) copy-start(bf16[96,512]{1,0:T(8,128)(2,1)S(1)} %collective-permute-done.10.up) | copy-start | bytes 294916
  37.7 9.6 %copy-start.3 = (bf16[96,512]{1,0:T(8,128)(2,1)}, bf16[96,512]{1,0:T(8,128)(2,1)S(1)}, u32[]{:S(2)}) copy-start(bf16[96,512]{1,0:T(8,128)(2,1)S(1)} %collective-permute-done.11.down) | copy-start | bytes 294916
  37.7 9.5 %collective-permute-start.12 = (bf16[96,512]{1,0:T(8,128)(2,1)S(1)}, bf16[96,512]{1,0:T(8,128)(2,1)S(1)}, u32[]{:S(2)}, u32[]{:S(2)}) collective-permute-start(bf16[96,512]{1,0:T(8,128)(2,1)S(1)} %pad_maximum_fusion.2), channel_id=1, source_target_pairs={{0,1},{1,2},{2,3},{3,4},{4,5},{5,6},{6,7},{7,8},{8,9},{9,10},{10,1... | collective-permute-start | bytes 294920 | tf_op jit(solution)/shard_map/ppermute | solution.py:66
  37.8 9.4 %collective-permute-start.13 = (bf16[96,512]{1,0:T(8,128)(2,1)S(1)}, bf16[96,512]{1,0:T(8,128)(2,1)S(1)}, u32[]{:S(2)}, u32[]{:S(2)}) collective-permute-start(bf16[96,512]{1,0:T(8,128)(2,1)S(1)} %pad_maximum_fusion.3), channel_id=1, source_target_pairs={{0,127},{1,0},{2,1},{3,2},{4,3},{5,4},{6,5},{7,6},{8,7},{9,8},{10,... | collective-permute-start | bytes 294920 | tf_op jit(solution)/shard_map/ppermute | solution.py:69
  47.3 0.6 copy-start.5
  47.3 0.7 copy-start.6
  47.3 1.0 %copy-start.1 = (bf16[1024,512]{1,0:T(8,128)(2,1)}, bf16[1024,512]{1,0:T(8,128)(2,1)S(1)}, u32[]{:S(2)}) copy-start(bf16[1024,512]{1,0:T(8,128)(2,1)S(1)} %collective-permute-done.9.other) | copy-start | bytes 3145732
